TPU v7x, 128 devices: a whole 4x4x4 slice. The times are simulated.
128 devices in a mesh: dp: 4 (over x_lo, core), tensor: 32 (over y, x_hi, z).
Axes of the slice: x: 4 (x_hi: 2, x_lo: 2; x = x_hi * 2 + x_lo), y: 4, z: 4, core: 2. Of those that a mesh axis runs over, the one named last changes fastest.
Arguments:
- qkv_master: float32 [7168, 21504], P(('dp', 'tensor')), may hold values from -0.0625 to 0.0625
- adapter_down: float32 [13, 7168, 128], P(None, ('dp', 'tensor')), may hold values from -0.0625 to 0.0625
- adapter_up: float32 [13, 128, 21504], P(None, None, 'tensor'), may hold values from -0.5 to 0.5
- adapter_pick: int32 [1], replicated, may hold values from 0 to 12
- out_master: float32 [3584, 7168], P(('dp', 'tensor')), may hold values from -0.0625 to 0.0625
- norm_gain: float32 [7168], replicated, may hold values from 0.1 to 1.9
- hidden_in: bfloat16 [2048, 3584], P(('dp', 'tensor')), may hold values from -6 to 6
- embed_in: bfloat16 [2048, 3584], P(('dp', 'tensor')), may hold values from -6 to 6
- prompt_len: int32 [4, 2], P('dp'), may hold values from 1 to 511, as said below
- prefix_len: int32 [4, 2], P('dp'), may hold values from 0 to 512, as said below
- prefix_holder: int32 [4, 2], P('dp'), may hold values from 0 to 3
- prefix_keys: bfloat16 [4, 512, 7168], P('dp', None, 'tensor'), may hold values from -6 to 6
- prefix_values: bfloat16 [4, 512, 7168], P('dp', None, 'tensor'), may hold values from -6 to 6
Outputs:
- server_qkv: bfloat16 [7168, 21504], P(None, 'tensor')
- server_out: bfloat16 [3584, 7168], P(None, 'tensor')
- block_out: bfloat16 [2048, 3584], P(('dp', 'tensor'))
- new_keys: bfloat16 [2048, 7168], P('dp', 'tensor')
- new_values: bfloat16 [2048, 7168], P('dp', 'tensor')
Inputs may be any that keep to these rules, and one draw needn't show every extreme that they name: `prompt_len`: the two prompt lengths of a replica add up to 512. `prefix_len`: exactly half of all requests extend a cached prefix (a positive length); the others have 0.
All inputs are finite; a program needn't handle non-finite values.
Results may differ from a plain program's by a relative error of at most 0.033.
Values may be sent and summed in bfloat16 or wider, within the bound.
A program may use at most 128 MiB of HBM per device.

v0:
```python
import math
import jax
import jax.numpy as jnp
from jax import lax
from jax.sharding import PartitionSpec as P


def partial_attention(queries, key_rows, value_rows, allowed, inv_scale):
    scores = (
        lax.dot_general(
            queries, key_rows, (((1,), (1,)), ((), ())), preferred_element_type=jnp.float32
        )
        * inv_scale
    )
    weights = jnp.where(allowed, jnp.exp(scores), jnp.float32(0.0))
    numerator = jnp.dot(
        weights.astype(jnp.bfloat16), value_rows, preferred_element_type=jnp.float32
    )
    return (numerator, jnp.sum(weights, axis=1))


def regroup_rows(columns, n_tensor, n_replica):
    col_count = columns.shape[1]
    row_count = columns.shape[0] // (n_tensor * n_replica)
    shaped = columns.reshape(n_tensor, n_replica, row_count, col_count)
    return jnp.transpose(shaped, (1, 0, 2, 3)).reshape(n_tensor * n_replica * row_count, col_count)


def body(
    qkv_master,
    adapter_down,
    adapter_up,
    adapter_pick,
    out_master,
    norm_gain,
    hidden_in,
    embed_in,
    prompt_len,
    prefix_len,
    prefix_holder,
    prefix_keys,
    prefix_values,
):
    n_tensor = lax.axis_size("tensor")
    n_replica = lax.axis_size("dp")
    chosen = adapter_pick[0]
    down_pick = lax.dynamic_index_in_dim(adapter_down, chosen, 0, keepdims=False).astype(
        jnp.bfloat16
    )
    up_pick = lax.dynamic_index_in_dim(adapter_up, chosen, 0, keepdims=False).astype(jnp.bfloat16)
    joined = jnp.concatenate([hidden_in, embed_in], axis=1).astype(jnp.float32)
    factor = lax.rsqrt(jnp.mean(joined * joined, axis=1, keepdims=True) + 1e-05)
    normed = (joined * factor * norm_gain).astype(jnp.bfloat16)
    all_rows, up_full = (
        lax.all_gather(normed, "tensor", axis=0, tiled=True),
        lax.all_gather(up_pick, "tensor", axis=1, tiled=True),
    )
    merged_qkv = (
        qkv_master + jnp.dot(down_pick, up_full, preferred_element_type=jnp.float32)
    ).astype(jnp.bfloat16)
    out_low = out_master.astype(jnp.bfloat16)
    rows_qkv, rows_out = (
        lax.all_gather(merged_qkv, "dp", axis=0, tiled=True),
        lax.all_gather(out_low, "dp", axis=0, tiled=True),
    )
    cols_qkv, cols_out = (
        lax.all_to_all(rows_qkv, "tensor", split_axis=1, concat_axis=0, tiled=True),
        lax.all_to_all(rows_out, "tensor", split_axis=1, concat_axis=0, tiled=True),
    )
    server_qkv = regroup_rows(cols_qkv, n_tensor, n_replica)
    server_out = regroup_rows(cols_out, n_tensor, n_replica)
    qkv_rows = jnp.dot(all_rows, server_qkv, preferred_element_type=jnp.float32).astype(
        jnp.bfloat16
    )
    head_size = qkv_rows.shape[1] // 3
    token_count = qkv_rows.shape[0]
    queries = qkv_rows[:, :head_size]
    new_keys = qkv_rows[:, head_size : 2 * head_size]
    new_values = qkv_rows[:, 2 * head_size :]
    inv_scale = 1.0 / math.sqrt(head_size)
    positions = jnp.arange(token_count, dtype=jnp.int32)
    lengths = prompt_len[0]
    request = (positions >= lengths[0]).astype(jnp.int32)
    block_rows = math.gcd(token_count, 512)
    first_row = 0
    last_row = first_row + block_rows
    allowed = (request[first_row:last_row, None] == request[None, :]) & (
        positions[None, :] <= positions[first_row:last_row, None]
    )
    numerator, weight_sum = partial_attention(queries, new_keys, new_values, allowed, inv_scale)
    own_parts = numerator
    own_sums = weight_sum
    cached_len = prefix_len[0]
    holders = prefix_holder[0]
    row_holder = jnp.where(request == 1, holders[1], holders[0])
    row_limit = jnp.where(request == 1, cached_len[1], cached_len[0])
    slot_ids = jnp.arange(prefix_keys.shape[1], dtype=jnp.int32)
    offset = jnp.int32(0)
    numerator = own_parts
    weight_sum = own_sums
    key_piece = lax.all_gather(prefix_keys, "dp", axis=0, tiled=True)
    value_piece = lax.all_gather(prefix_values, "dp", axis=0, tiled=True)
    for member in range(key_piece.shape[0]):
        replica = offset + member
        first_row = 0
        last_row = first_row + block_rows
        usable = (row_holder[first_row:last_row, None] == replica) & (
            slot_ids[None, :] < row_limit[first_row:last_row, None]
        )
        part_num, part_sum = partial_attention(
            queries, key_piece[member], value_piece[member], usable, inv_scale
        )
        numerator = numerator + part_num
        weight_sum = weight_sum + part_sum
    numerator, weight_sum = (numerator, weight_sum)
    attention = (numerator / weight_sum[:, None]).astype(jnp.bfloat16)
    block_out = lax.psum_scatter(
        lax.dot_general(
            attention, server_out, (((1,), (1,)), ((), ())), preferred_element_type=jnp.float32
        ).astype(jnp.bfloat16),
        "tensor",
        scatter_dimension=0,
        tiled=True,
    )
    return (server_qkv, server_out, block_out, new_keys, new_values)


def solution(mesh):
    in_specs = (
        P(("dp", "tensor"), None),
        P(None, ("dp", "tensor"), None),
        P(None, None, "tensor"),
        P(),
        P(("dp", "tensor"), None),
        P(),
        P(("dp", "tensor"), None),
        P(("dp", "tensor"), None),
        P("dp", None),
        P("dp", None),
        P("dp", None),
        P("dp", None, "tensor"),
        P("dp", None, "tensor"),
    )
    out_specs = (
        P(None, "tensor"),
        P(None, "tensor"),
        P(("dp", "tensor"), None),
        P("dp", "tensor"),
        P("dp", "tensor"),
    )
    return jax.shard_map(body, mesh=mesh, in_specs=in_specs, out_specs=out_specs, check_vma=False)
```

profile of v0, /device:TPU:0, one launch (start us, length us, event | category | flops | bytes accessed | tf_op | source)
XLA Modules:
  0.0 744.3 jit_solution(5909597050961547122)
XLA Ops:
  7.9 1.7 dynamic-slice_convert_fusion
  9.7 2.0 convert_bitcast_fusion
  11.8 90.2 %all-gather.11.cloned.1.call-done = bf16[1,128,21504]{1,2,0:T(8,128)(2,1)} async-done(((bf16[1,128,672]{1,2,0:T(8,128)(2,1)}), bf16[1,128,21504]{1,2,0:T(8,128)(2,1)}) %all-gather.11.cloned.1.call-update) | async-done | bytes 5505040 | tf_op jit(solution)/shard_map/all_gather | solution.py:56
  101.9 8.7 %fusion = bf16[56,21504]{1,0:T(8,128)(2,1)} fusion(f32[56,21504]{1,0:T(8,128)} %param.13, bf16[1,128,21504]{1,2,0:T(8,128)(2,1)} %all-gather.11.cloned.1.call-done, f32[13,56,128]{2,1,0:T(8,128)S(1)} %copy-done, s32[]{:T(128)S(6)} %select_n.46), kind=kOutput, calls=%fused_computation.1 | convolution fusion | flops 310689792 | bytes 12744708 | tf_op jit(solution)/shard_map/dot_general | solution.py:59
  111.0 0.8 fusion.28
  111.8 17.1 %all-gather.13.cloned.1.call-done = bf16[4,28,7168]{2,1,0:T(8,128)(2,1)} async-done(((bf16[1,28,7168]{2,1,0:T(8,128)(2,1)}), bf16[4,28,7168]{2,1,0:T(8,128)(2,1)}) %all-gather.13.cloned.1.call-update) | async-done | bytes 1605648 | tf_op jit(solution)/shard_map/all_gather | solution.py:64
  128.9 3.7 all_to_all.27
  132.6 2.3 copy.29
  134.9 9.4 %all-to-all-start.1 = ((bf16[112,32,224]{2,0,1:T(8,128)(2,1)}), bf16[112,32,224]{2,0,1:T(8,128)(2,1)S(1)}, u32[]{:S(2)}, u32[]{:S(2)}) async-start(bf16[112,32,224]{2,0,1:T(8,128)(2,1)} %copy.29), calls=%async_computation.1 | async-start | bytes 3670016 | tf_op jit(solution)/shard_map/all_to_all | solution.py:68
  144.3 97.9 %all-gather.7.cloned.1.call-done = bf16[224,21504]{1,0:T(8,128)(2,1)} async-done(((bf16[56,21504]{1,0:T(8,128)(2,1)}), bf16[224,21504]{1,0:T(8,128)(2,1)}) %all-gather.7.cloned.1.call-update) | async-done | bytes 9633808 | tf_op jit(solution)/shard_map/all_gather | solution.py:63
  242.2 20.8 %all_to_all.24 = bf16[224,32,672]{2,1,0:T(8,128)(2,1)} reshape(bf16[224,21504]{1,0:T(8,128)(2,1)} %all-gather.7.cloned.1.call-done) | data formatting | bytes 19267584 | tf_op jit(solution)/shard_map/all_to_all | solution.py:67
  263.1 11.6 %copy.27 = bf16[224,32,672]{2,0,1:T(8,128)(2,1)} copy(bf16[224,32,672]{2,1,0:T(8,128)(2,1)} %all_to_all.24) | data formatting | bytes 19267584 | tf_op jit(solution)/shard_map/all_to_all | solution.py:67
  274.8 10.4 %all-to-all-start = ((bf16[224,32,672]{2,0,1:T(8,128)(2,1)}), bf16[224,32,672]{2,0,1:T(8,128)(2,1)}, u32[]{:S(2)}, u32[]{:S(2)}) async-start(bf16[224,32,672]{2,0,1:T(8,128)(2,1)} %copy.27), calls=%async_computation | async-start | bytes 22020096 | tf_op jit(solution)/shard_map/all_to_all | solution.py:67
  285.2 0.6 fusion.40
  285.8 1.3 select_compare_fusion
  287.1 1.3 select_compare_fusion.2
  288.5 0.6 fusion.41
  289.1 1.3 broadcast_select_fusion
  290.4 194.6 %all_gather.22 = bf16[4,512,224]{1,2,0:T(8,128)(2,1)} all-gather(bf16[1,512,224]{1,2,0:T(8,128)(2,1)S(1)} %copy-done.7), channel_id=1, replica_groups=mesh['dp'=4,'tensor'=32] {'dp'}, dimensions={0}, use_global_device_ids=true | all-gather | bytes 1146880 | tf_op jit(solution)/shard_map/all_gather | solution.py:101
  485.0 11.8 %all_gather.23 = bf16[4,512,224]{1,2,0:T(8,128)(2,1)S(1)} all-gather(bf16[1,512,224]{1,2,0:T(8,128)(2,1)S(1)} %copy-done.8), channel_id=1, replica_groups=mesh['dp'=4,'tensor'=32] {'dp'}, dimensions={0}, use_global_device_ids=true | all-gather | bytes 1146880 | tf_op jit(solution)/shard_map/all_gather | solution.py:102
  496.8 0.7 copy.30
  497.4 2.4 copy.31
  499.8 2.8 reshape.99
  502.6 9.8 %copy.28 = bf16[4,32,56,672]{3,2,1,0:T(8,128)(2,1)} copy(bf16[4,32,56,672]{3,2,0,1:T(8,128)(2,1)} %bitcast.5) | data formatting | bytes 19267584 | tf_op jit(solution)/shard_map/transpose | solution.py:26
  512.5 13.6 %convolution_convert_fusion.1 = bf16[512,672]{0,1:T(8,128)(2,1)S(1)} fusion(bf16[512,7168]{1,0:T(8,128)(2,1)} %all-gather.9.cloned.1.call-done, bf16[7168,672]{1,0:T(8,128)(2,1)} %bitcast.72), kind=kOutput, calls=%fused_computation.19 | convolution fusion | flops 4932845568 | bytes 17661952 | tf_op jit(solution)/shard_map/dot_general | solution.py:72
  526.1 1.3 fusion.42
  528.5 0.5 fusion.46
  530.4 1.1 convolution_add_fusion.2
  531.5 4.6 convolution_convert_fusion
  536.1 2.5 copy.33
  538.6 13.5 %copy.32 = bf16[7168,672]{0,1:T(8,128)(2,1)} copy(bf16[7168,672]{1,0:T(8,128)(2,1)} %bitcast.73) | data formatting | bytes 19267584
  552.0 185.8 %reduce-scatter.2.cloned.1.call-done = bf16[16,3584]{1,0:T(8,128)(2,1)} async-done(((bf16[512,3584]{1,0:T(8,128)(2,1)}), bf16[16,3584]{1,0:T(8,128)(2,1)}) %reduce-scatter.2.cloned.1.call-update) | async-done | bytes 114704 | tf_op jit(solution)/shard_map/reduce_scatter | solution.py:117
  (50 shorter events, 3.0 us)
Async XLA Ops:
  7.2 94.8 %copy-start = (f32[13,56,128]{2,1,0:T(8,128)S(1)}, f32[13,56,128]{2,1,0:T(8,128)}, u32[]{:S(2)}) copy-start(f32[13,56,128]{2,1,0:T(8,128)} %param.14) | copy-start | bytes 1118212
  7.2 94.7 %all-gather.11.cloned.1.call-start = ((), (), s32[]{:S(2)}) async-start(), calls=%async_computation.6 | async-start | bytes 5677056 | tf_op jit(solution)/shard_map/all_gather | solution.py:56
  9.6 119.3 %all-gather.13.cloned.1.call-start = ((), (), s32[]{:S(2)}) async-start(), calls=%async_computation.7 | async-start | bytes 2293760 | tf_op jit(solution)/shard_map/all_gather | solution.py:64
  11.7 99.1 %copy-start.4 = (bf16[16,3584]{1,0:T(8,128)(2,1)S(1)}, bf16[16,3584]{1,0:T(8,128)(2,1)}, u32[]{:S(2)}) copy-start(bf16[16,3584]{1,0:T(8,128)(2,1)} %param.20) | copy-start | bytes 344068
  11.7 99.1 %copy-start.5 = (bf16[16,3584]{1,0:T(8,128)(2,1)S(1)}, bf16[16,3584]{1,0:T(8,128)(2,1)}, u32[]{:S(2)}) copy-start(bf16[16,3584]{1,0:T(8,128)(2,1)} %param.19) | copy-start | bytes 344068
  11.7 99.2 %copy-start.9 = (f32[7168]{0:T(1024)S(1)}, f32[7168]{0:T(1024)}, u32[]{:S(2)}) copy-start(f32[7168]{0:T(1024)} %param.18) | copy-start | bytes 86020
  11.7 230.5 %all-gather.7.cloned.1.call-start = ((), (), s32[]{:S(2)}) async-start(), calls=%async_computation.3 | async-start | bytes 12042240 | tf_op jit(solution)/shard_map/all_gather | solution.py:63
  110.7 401.8 %all-gather.9.cloned.1.call-start = ((), (), s32[]{:S(2)}) async-start(), calls=%async_computation.4 | async-start | bytes 7569408 | tf_op jit(solution)/shard_map/all_gather | solution.py:55
  134.9 139.8 %all-to-all-start.1 = ((bf16[112,32,224]{2,0,1:T(8,128)(2,1)}), bf16[112,32,224]{2,0,1:T(8,128)(2,1)S(1)}, u32[]{:S(2)}, u32[]{:S(2)}) async-start(bf16[112,32,224]{2,0,1:T(8,128)(2,1)} %copy.29), calls=%async_computation.1 | async-start | bytes 3670016 | tf_op jit(solution)/shard_map/all_to_all | solution.py:68
  274.7 10.5 %copy-start.11 = (s32[1,2]{1,0:T(1,128)S(1)}, s32[1,2]{1,0:T(1,128)}, u32[]{:S(2)}) copy-start(s32[1,2]{1,0:T(1,128)} %param.23) | copy-start | bytes 28
  274.7 11.1 %copy-start.10 = (s32[1,2]{1,0:T(1,128)S(1)}, s32[1,2]{1,0:T(1,128)}, u32[]{:S(2)}) copy-start(s32[1,2]{1,0:T(1,128)} %param.21) | copy-start | bytes 28
  274.7 13.8 %copy-start.12 = (s32[1,2]{1,0:T(1,128)S(1)}, s32[1,2]{1,0:T(1,128)}, u32[]{:S(2)}) copy-start(s32[1,2]{1,0:T(1,128)} %param.22) | copy-start | bytes 28
  274.7 15.7 %copy-start.7 = (bf16[1,512,224]{1,2,0:T(8,128)(2,1)S(1)}, bf16[1,512,224]{1,2,0:T(8,128)(2,1)}, u32[]{:S(2)}) copy-start(bf16[1,512,224]{1,2,0:T(8,128)(2,1)} %param.24) | copy-start | bytes 688132
  274.7 210.2 %copy-start.8 = (bf16[1,512,224]{1,2,0:T(8,128)(2,1)S(1)}, bf16[1,512,224]{1,2,0:T(8,128)(2,1)}, u32[]{:S(2)}) copy-start(bf16[1,512,224]{1,2,0:T(8,128)(2,1)} %param.25) | copy-start | bytes 688132
  274.8 227.9 %all-to-all-start = ((bf16[224,32,672]{2,0,1:T(8,128)(2,1)}), bf16[224,32,672]{2,0,1:T(8,128)(2,1)}, u32[]{:S(2)}, u32[]{:S(2)}) async-start(bf16[224,32,672]{2,0,1:T(8,128)(2,1)} %copy.27), calls=%async_computation | async-start | bytes 22020096 | tf_op jit(solution)/shard_map/all_to_all | solution.py:67
  285.2 452.6 %reduce-scatter.2.cloned.1.call-start = ((), (), s32[]{:S(2)}) async-start(), calls=%async_computation.5 | async-start | bytes 3784704 | tf_op jit(solution)/shard_map/reduce_scatter | solution.py:117
  512.5 13.6 %copy-start.3 = (bf16[4,512,224]{1,2,0:T(8,128)(2,1)S(1)}, bf16[4,512,224]{1,2,0:T(8,128)(2,1)}, u32[]{:S(2)}) copy-start(bf16[4,512,224]{1,2,0:T(8,128)(2,1)} %all_gather.22) | copy-start | bytes 2752516
  526.1 3.0 copy-start.6
  526.1 3.4 copy-start.2
  538.6 199.3 %copy-start.1 = (f32[13,56,128]{2,1,0:T(8,128)S(1)}, f32[13,56,128]{2,1,0:T(8,128)}, u32[]{:S(2)}) copy-start(f32[13,56,128]{2,1,0:T(8,128)} %param.14) | copy-start | bytes 1118212
Sparse Core Ops, SparseCore 0:
  11.6 90.2 all-gather.10
  104.2 24.7 all-gather.12
  131.2 111.0 all-gather.6
  245.7 228.1 all-gather.8
  536.2 201.5 reduce-scatter.1
where the time goes:
time: 746 us; the launch traced here: 744 us
  waiting for transfers between devices  391 us (52%)
  blocking collectives  206 us (28%)
  local copies, waits for them, and re-layouts  73 us (10%)
  matrix products  32.2 us (4%)
  starting transfers between devices  20 us (3%)
  between operations  14.7 us (2%)
    all_gather x1, blocking collectives, body(): key_piece = lax.all_gather(prefix_keys, 'dp', axis=0, tiled=True)  195 us
    reduce_scatter x1, waiting for transfers between devices, body(): lax.psum_scatter(lax.dot_general(attention, server_out, (((1,), (1,)), ((...  186 us
    all_gather x1, waiting for transfers between devices, body(): lax.all_gather(merged_qkv, 'dp', axis=0, tiled=True)  97.9 us
    all_gather x1, waiting for transfers between devices, body(): lax.all_gather(up_pick, 'tensor', axis=1, tiled=True)  90.2 us
    all_to_all x2, local copies, waits for them, and re-layouts, body(): lax.all_to_all(rows_qkv, 'tensor', split_axis=1, concat_axis=0, tiled=True)  32.5 us
    all_gather x1, waiting for transfers between devices, body(): lax.all_gather(out_low, 'dp', axis=0, tiled=True)  17.1 us
    unnamed x28, local copies, waits for them, and re-layouts  16 us
  transfers between devices with their start and end apart: 7, of which 4 were waited for; matrix products, arithmetic and copies ran while one was open for 8% of the time, Pallas kernels for 0%

commit v1 on v0

--- a/solution.py
+++ b/solution.py
@@ -61,7 +61,9 @@
     out_low = out_master.astype(jnp.bfloat16)
     rows_qkv, rows_out = (
         lax.all_gather(merged_qkv, "dp", axis=0, tiled=True),
-        lax.all_gather(out_low, "dp", axis=0, tiled=True),
+        jnp.concatenate(
+            lax.all_to_all(jnp.stack([out_low] * lax.axis_size("dp")), "dp", 0, 0), axis=0
+        ),
     )
     cols_qkv, cols_out = (
         lax.all_to_all(rows_qkv, "tensor", split_axis=1, concat_axis=0, tiled=True),

time: 746 us -> 734 us (0.984)
  waiting for transfers between devices: 391 us -> 348 us
  blocking collectives: 206 us -> 247 us
  starting transfers between devices: 20 us -> 11.5 us
    all_to_all x0 -> x1, blocking collectives: none -> 39.4 us  [body(): lax.all_to_all(jnp.stack([out_low] * lax.axis_size('dp')), 'dp', 0, 0)]
    all_gather x1, waiting for transfers between devices: 97.9 us -> 70.7 us  [body(): lax.all_gather(merged_qkv, 'dp', axis=0, tiled=True)]
    all_gather x1 -> x0, waiting for transfers between devices: 17.1 us -> none  [body(): lax.all_gather(out_low, 'dp', axis=0, tiled=True)]
    unnamed x28 -> x30, local copies, waits for them, and re-layouts: 16 us -> 16 us
  transfers between devices with their start and end apart: 7 -> 6, of which waited for: 4 -> 3; matrix products, arithmetic and copies ran while one was open for 8% -> 7% of each run, Pallas kernels for 0% -> 0%
where the time goes in v1:
time: 734 us; the launch traced here: 733 us
  waiting for transfers between devices  348 us (47%)
  blocking collectives  247 us (34%)
  local copies, waits for them, and re-layouts  74.4 us (10%)
  matrix products  32.1 us (4%)
  between operations  14.7 us (2%)
  starting transfers between devices  11.5 us (2%)
    all_gather x1, blocking collectives, body(): key_piece = lax.all_gather(prefix_keys, 'dp', axis=0, tiled=True)  196 us
    reduce_scatter x1, waiting for transfers between devices, body(): lax.psum_scatter(lax.dot_general(attention, server_out, (((1,), (1,)), ((...  185 us
    all_gather x1, waiting for transfers between devices, body(): lax.all_gather(up_pick, 'tensor', axis=1, tiled=True)  92.2 us
    all_gather x1, waiting for transfers between devices, body(): lax.all_gather(merged_qkv, 'dp', axis=0, tiled=True)  70.7 us
    all_to_all x1, blocking collectives, body(): lax.all_to_all(jnp.stack([out_low] * lax.axis_size('dp')), 'dp', 0, 0)  39.4 us
    all_to_all x2, local copies, waits for them, and re-layouts, body(): lax.all_to_all(rows_qkv, 'tensor', split_axis=1, concat_axis=0, tiled=True)  32.3 us
    unnamed x30, local copies, waits for them, and re-layouts  16 us
  transfers between devices with their start and end apart: 6, of which 3 were waited for; matrix products, arithmetic and copies ran while one was open for 7% of the time, Pallas kernels for 0%

profile of v1, /device:TPU:0, one launch (start us, length us, event | category | flops | bytes accessed | tf_op | source)
XLA Modules:
  0.0 732.9 jit_solution(4200196415977189575)
XLA Ops:
  7.9 1.7 dynamic-slice_convert_fusion
  9.7 92.2 %all-gather.9.cloned.1.call-done = bf16[1,128,21504]{1,2,0:T(8,128)(2,1)} async-done(((bf16[1,128,672]{1,2,0:T(8,128)(2,1)}), bf16[1,128,21504]{1,2,0:T(8,128)(2,1)}) %all-gather.9.cloned.1.call-update) | async-done | bytes 5505040 | tf_op jit(solution)/shard_map/all_gather | solution.py:56
  101.9 8.7 %fusion = bf16[56,21504]{1,0:T(8,128)(2,1)} fusion(f32[56,21504]{1,0:T(8,128)} %param.13, bf16[1,128,21504]{1,2,0:T(8,128)(2,1)} %all-gather.9.cloned.1.call-done, f32[13,56,128]{2,1,0:T(8,128)S(1)} %copy-done, s32[]{:T(128)S(6)} %select_n.46), kind=kOutput, calls=%fused_computation.1 | convolution fusion | flops 310689792 | bytes 12744708 | tf_op jit(solution)/shard_map/dot_general | solution.py:59
  110.9 0.8 fusion.28
  112.0 39.4 %all_to_all.37 = bf16[4,28,7168]{2,1,0:T(8,128)(2,1)S(1)} all-to-all(bf16[4,28,7168]{2,1,0:T(8,128)(2,1)S(1)} %stack.2), channel_id=1, replica_groups=mesh['dp'=4,'tensor'=32] {'dp'}, dimensions={0} | all-to-all | bytes 3211264 | tf_op jit(solution)/shard_map/all_to_all | solution.py:65
  151.4 3.6 all_to_all.31
  155.0 3.8 copy.29
  158.7 4.7 all-to-all-start.2
  163.5 70.7 %all-gather.5.cloned.1.call-done = bf16[224,21504]{1,0:T(8,128)(2,1)} async-done(((bf16[56,21504]{1,0:T(8,128)(2,1)}), bf16[224,21504]{1,0:T(8,128)(2,1)}) %all-gather.5.cloned.1.call-update) | async-done | bytes 9633808 | tf_op jit(solution)/shard_map/all_gather | solution.py:63
  234.2 20.8 %all_to_all.27 = bf16[224,32,672]{2,1,0:T(8,128)(2,1)} reshape(bf16[224,21504]{1,0:T(8,128)(2,1)} %all-gather.5.cloned.1.call-done) | data formatting | bytes 19267584 | tf_op jit(solution)/shard_map/all_to_all | solution.py:69
  255.1 11.5 %copy.27 = bf16[224,32,672]{2,0,1:T(8,128)(2,1)} copy(bf16[224,32,672]{2,1,0:T(8,128)(2,1)} %all_to_all.27) | data formatting | bytes 19267584 | tf_op jit(solution)/shard_map/all_to_all | solution.py:69
  266.6 6.6 all-to-all-start
  273.3 0.6 fusion.40
  273.9 1.3 select_compare_fusion
  275.2 1.3 select_compare_fusion.2
  276.6 0.6 fusion.41
  277.1 1.3 broadcast_select_fusion
  278.5 196.1 %all_gather.18 = bf16[4,512,224]{1,2,0:T(8,128)(2,1)} all-gather(bf16[1,512,224]{1,2,0:T(8,128)(2,1)S(1)} %copy-done.8), channel_id=1, replica_groups=mesh['dp'=4,'tensor'=32] {'dp'}, dimensions={0}, use_global_device_ids=true | all-gather | bytes 1146880 | tf_op jit(solution)/shard_map/all_gather | solution.py:103
  474.6 11.8 %all_gather.19 = bf16[4,512,224]{1,2,0:T(8,128)(2,1)S(1)} all-gather(bf16[1,512,224]{1,2,0:T(8,128)(2,1)S(1)} %copy-done.9), channel_id=1, replica_groups=mesh['dp'=4,'tensor'=32] {'dp'}, dimensions={0}, use_global_device_ids=true | all-gather | bytes 1146880 | tf_op jit(solution)/shard_map/all_gather | solution.py:104
  486.4 0.7 copy.30
  487.0 2.4 copy.31
  489.4 2.8 reshape.103
  492.2 9.8 %copy.28 = bf16[4,32,56,672]{3,2,1,0:T(8,128)(2,1)} copy(bf16[4,32,56,672]{3,2,0,1:T(8,128)(2,1)} %bitcast.5) | data formatting | bytes 19267584 | tf_op jit(solution)/shard_map/transpose | solution.py:26
  502.1 13.6 %convolution_convert_fusion.1 = bf16[512,672]{0,1:T(8,128)(2,1)S(1)} fusion(bf16[512,7168]{1,0:T(8,128)(2,1)} %all-gather.7.cloned.1.call-done, bf16[7168,672]{1,0:T(8,128)(2,1)} %bitcast.70), kind=kOutput, calls=%fused_computation.19 | convolution fusion | flops 4932845568 | bytes 17661952 | tf_op jit(solution)/shard_map/dot_general | solution.py:74
  515.7 1.3 fusion.42
  517.0 0.5 fusion.43
  517.6 0.5 fusion.44
  520.0 1.1 convolution_add_fusion.2
  521.0 4.6 convolution_convert_fusion
  525.6 2.5 copy.33
  528.1 13.5 %copy.32 = bf16[7168,672]{0,1:T(8,128)(2,1)} copy(bf16[7168,672]{1,0:T(8,128)(2,1)} %bitcast.71) | data formatting | bytes 19267584
  541.6 184.8 %reduce-scatter.2.cloned.1.call-done = bf16[16,3584]{1,0:T(8,128)(2,1)} async-done(((bf16[512,3584]{1,0:T(8,128)(2,1)}), bf16[16,3584]{1,0:T(8,128)(2,1)}) %reduce-scatter.2.cloned.1.call-update) | async-done | bytes 114704 | tf_op jit(solution)/shard_map/reduce_scatter | solution.py:119
  (51 shorter events, 2.6 us)
Async XLA Ops:
  7.2 94.8 %copy-start = (f32[13,56,128]{2,1,0:T(8,128)S(1)}, f32[13,56,128]{2,1,0:T(8,128)}, u32[]{:S(2)}) copy-start(f32[13,56,128]{2,1,0:T(8,128)} %param.14) | copy-start | bytes 1118212
  7.2 94.7 %all-gather.9.cloned.1.call-start = ((), (), s32[]{:S(2)}) async-start(), calls=%async_computation.7 | async-start | bytes 5677056 | tf_op jit(solution)/shard_map/all_gather | solution.py:56
  9.6 101.1 %copy-start.5 = (bf16[16,3584]{1,0:T(8,128)(2,1)S(1)}, bf16[16,3584]{1,0:T(8,128)(2,1)}, u32[]{:S(2)}) copy-start(bf16[16,3584]{1,0:T(8,128)(2,1)} %param.20) | copy-start | bytes 344068
  9.6 101.1 %copy-start.6 = (bf16[16,3584]{1,0:T(8,128)(2,1)S(1)}, bf16[16,3584]{1,0:T(8,128)(2,1)}, u32[]{:S(2)}) copy-start(bf16[16,3584]{1,0:T(8,128)(2,1)} %param.19) | copy-start | bytes 344068
  9.6 101.3 %copy-start.10 = (f32[7168]{0:T(1024)S(1)}, f32[7168]{0:T(1024)}, u32[]{:S(2)}) copy-start(f32[7168]{0:T(1024)} %param.18) | copy-start | bytes 86020
  9.6 102.1 %copy-start.3 = (f32[28,7168]{1,0:T(8,128)S(1)}, f32[28,7168]{1,0:T(8,128)}, u32[]{:S(2)}) copy-start(f32[28,7168]{1,0:T(8,128)} %param.17) | copy-start | bytes 2408452
  9.7 224.6 %all-gather.5.cloned.1.call-start = ((), (), s32[]{:S(2)}) async-start(), calls=%async_computation.4 | async-start | bytes 12042240 | tf_op jit(solution)/shard_map/all_gather | solution.py:63
  110.7 391.4 %all-gather.7.cloned.1.call-start = ((), (), s32[]{:S(2)}) async-start(), calls=%async_computation.5 | async-start | bytes 7569408 | tf_op jit(solution)/shard_map/all_gather | solution.py:55
  158.7 107.8 %all-to-all-start.2 = ((bf16[112,32,224]{2,0,1:T(8,128)(2,1)}), bf16[112,32,224]{2,0,1:T(8,128)(2,1)S(1)}, u32[]{:S(2)}, u32[]{:S(2)}) async-start(bf16[112,32,224]{2,0,1:T(8,128)(2,1)} %copy.29), calls=%async_computation.2 | async-start | bytes 3670016 | tf_op jit(solution)/shard_map/all_to_all | solution.py:70
  266.6 6.7 copy-start.12
  266.6 7.3 copy-start.11
  266.6 10.0 %copy-start.13 = (s32[1,2]{1,0:T(1,128)S(1)}, s32[1,2]{1,0:T(1,128)}, u32[]{:S(2)}) copy-start(s32[1,2]{1,0:T(1,128)} %param.22) | copy-start | bytes 28
  266.6 11.9 %copy-start.8 = (bf16[1,512,224]{1,2,0:T(8,128)(2,1)S(1)}, bf16[1,512,224]{1,2,0:T(8,128)(2,1)}, u32[]{:S(2)}) copy-start(bf16[1,512,224]{1,2,0:T(8,128)(2,1)} %param.24) | copy-start | bytes 688132
  266.6 208.0 %copy-start.9 = (bf16[1,512,224]{1,2,0:T(8,128)(2,1)S(1)}, bf16[1,512,224]{1,2,0:T(8,128)(2,1)}, u32[]{:S(2)}) copy-start(bf16[1,512,224]{1,2,0:T(8,128)(2,1)} %param.25) | copy-start | bytes 688132
  266.6 225.6 %all-to-all-start = ((bf16[224,32,672]{2,0,1:T(8,128)(2,1)}), bf16[224,32,672]{2,0,1:T(8,128)(2,1)}, u32[]{:S(2)}, u32[]{:S(2)}) async-start(bf16[224,32,672]{2,0,1:T(8,128)(2,1)} %copy.27), calls=%async_computation | async-start | bytes 22020096 | tf_op jit(solution)/shard_map/all_to_all | solution.py:69
  273.2 453.1 %reduce-scatter.2.cloned.1.call-start = ((), (), s32[]{:S(2)}) async-start(), calls=%async_computation.6 | async-start | bytes 3784704 | tf_op jit(solution)/shard_map/reduce_scatter | solution.py:119
  502.1 13.6 %copy-start.4 = (bf16[4,512,224]{1,2,0:T(8,128)(2,1)S(1)}, bf16[4,512,224]{1,2,0:T(8,128)(2,1)}, u32[]{:S(2)}) copy-start(bf16[4,512,224]{1,2,0:T(8,128)(2,1)} %all_gather.18) | copy-start | bytes 2752516
  515.7 3.0 copy-start.7
  515.7 3.4 copy-start.2
  528.1 198.2 %copy-start.1 = (f32[13,56,128]{2,1,0:T(8,128)S(1)}, f32[13,56,128]{2,1,0:T(8,128)}, u32[]{:S(2)}) copy-start(f32[13,56,128]{2,1,0:T(8,128)} %param.14) | copy-start | bytes 1118212
Sparse Core Ops, SparseCore 0:
  11.6 90.2 all-gather.8
  110.8 123.3 all-gather.4
  237.8 226.8 all-gather.6
  525.8 200.5 reduce-scatter.1
